TPU v7x, 32 devices: a whole 2x2x4 slice. The times are simulated.
32 devices in a mesh: row: 4 (over y, x), col: 8 (over z, core).
Axes of the slice: x: 2, y: 2, z: 4, core: 2. Of those that a mesh axis runs over, the one named last changes fastest.
Arguments:
- panel_right: bfloat16 [32, 1536, 128], P('row', 'col'), may hold values from -1 to 1
- factor_inverse: bfloat16 [1536, 1536], replicated, as said below
- ranks: int32 [32], P(('row', 'col')), may hold values from 32 to 128
- owner_map: int32 [32], replicated, may hold values from 0 to 31, each once
- cores: float32 [4, 8, 8, 4, 128, 128], P('row', 'col'), may hold values from -6 to 6
Outputs:
- new_cores: float32 [4, 8, 8, 4, 128, 128], P('row', 'col')
Inputs may be any that keep to these rules, and one draw needn't show every extreme that they name: `factor_inverse`: lower triangular, the inverse of a Cholesky factor.
All inputs are finite; a program needn't handle non-finite values.
Results may differ from a plain program's by a relative error of at most 0.0033.
Values may be sent and summed in bfloat16 or wider, within the bound.
No kernel may reach another device: no remote copies, remote signals or barrier semaphores. Data moves between devices by JAX's collectives and lax.ppermute only.
A program may use at most 128 MiB of HBM per device.

v0:
```python
import jax
import jax.numpy as jnp
from jax import lax
from jax.sharding import PartitionSpec as P


def body(panel_right, factor_inverse, ranks, owner_map, cores):
    n_row = lax.axis_size("row")
    n_col = lax.axis_size("col")
    devices = n_row * n_col
    order = factor_inverse.shape[0]
    width = panel_right.shape[2]
    whole = lax.all_to_all(panel_right, "col", split_axis=0, concat_axis=1, tiled=True)
    solved = jnp.einsum("ij,bjk->bik", factor_inverse, whole, preferred_element_type=jnp.float32)
    column = lax.broadcasted_iota(jnp.int32, (1, 1, width), 2)
    keep = column < ranks.reshape(1, 1, 1)
    panel_left = jnp.where(keep, solved, 0.0).astype(jnp.bfloat16)
    pieces = panel_left.reshape(devices, order // devices, width)
    spread = lax.all_to_all(pieces, ("row", "col"), split_axis=0, concat_axis=0, tiled=True)
    moved = jnp.take(spread, owner_map, axis=0)
    back = lax.all_to_all(moved, ("row", "col"), split_axis=0, concat_axis=0, tiled=True)
    held = back.reshape(1, order, width)
    column_set = lax.all_gather(held, "row", axis=0, tiled=True)
    gram = jnp.einsum(
        "aik,bil->abkl",
        lax.all_gather(held, "col", axis=0, tiled=True),
        column_set,
        preferred_element_type=jnp.float32,
    )
    return cores - gram[None, None]


def solution(mesh):
    return jax.shard_map(
        body,
        mesh=mesh,
        in_specs=(
            P("row", "col", None),
            P(),
            P(("row", "col")),
            P(),
            P("row", "col", None, None, None, None),
        ),
        out_specs=P("row", "col", None, None, None, None),
        check_vma=False,
    )
```

profile of v0, /device:TPU:0, one launch (start us, length us, event | category | flops | bytes accessed | tf_op | source)
XLA Modules:
  0.0 147.6 jit_solution(1991811806430617758)
XLA Ops:
  6.5 6.4 %all-to-all-start = ((bf16[8,192,128]{2,1,0:T(8,128)(2,1)}), bf16[8,192,128]{2,1,0:T(8,128)(2,1)S(1)}, u32[]{:S(2)}, u32[]{:S(2)}) async-start(bf16[8,192,128]{2,1,0:T(8,128)(2,1)} %param.5), calls=%async_computation | async-start | bytes 786432 | tf_op jit(solution)/shard_map/all_to_all | solution.py:13
  13.6 11.9 %all-to-all-done = bf16[8,192,128]{2,1,0:T(8,128)(2,1)S(1)} async-done(((bf16[8,192,128]{2,1,0:T(8,128)(2,1)}), bf16[8,192,128]{2,1,0:T(8,128)(2,1)S(1)}, u32[]{:S(2)}, u32[]{:S(2)}) %all-to-all-start) | async-done | bytes 393248 | tf_op jit(solution)/shard_map/all_to_all | solution.py:13
  25.4 0.0 copy-start
  25.4 4.0 %fusion.4 = bf16[1,1536,128]{1,2,0:T(8,128)(2,1)S(1)} fusion(bf16[1536,128]{1,0:T(8,128)(2,1)S(1)} %bitcast.33, bf16[1536,1536]{1,0:T(8,128)(2,1)} %param.6, pred[128]{0:T(512)(128)(4,1)S(1)} %iota_compare_fusion), kind=kOutput, calls=%fused_computation.6 | convolution fusion | flops 604372992 | bytes 5505152 | tf_op jit(solution)/shard_map/ij,bjk->bik/dot_general | solution.py:14
  29.4 0.9 copy.14
  30.4 3.5 %all-to-all-start.1 = ((bf16[32,48,128]{2,1,0:T(8,128)(2,1)}), bf16[32,48,128]{2,1,0:T(8,128)(2,1)S(1)}, u32[]{:S(2)}, u32[]{:S(2)}) async-start(bf16[32,48,128]{2,1,0:T(8,128)(2,1)} %bitcast.4), calls=%async_computation.1 | async-start | bytes 786432 | tf_op jit(solution)/shard_map/all_to_all | solution.py:19
  33.9 0.0 all-gather.3.cloned.1.call-start
  34.0 0.0 copy-done
  34.0 13.3 %all-to-all-done.1 = bf16[32,48,128]{2,1,0:T(8,128)(2,1)S(1)} async-done(((bf16[32,48,128]{2,1,0:T(8,128)(2,1)}), bf16[32,48,128]{2,1,0:T(8,128)(2,1)S(1)}, u32[]{:S(2)}, u32[]{:S(2)}) %all-to-all-start.1) | async-done | bytes 393248 | tf_op jit(solution)/shard_map/all_to_all | solution.py:19
  47.3 0.6 gather_fusion
  48.0 0.1 broadcast_select_fusion
  48.1 15.8 %all_to_all.19 = bf16[32,48,128]{2,1,0:T(8,128)(2,1)} all-to-all(bf16[32,48,128]{2,1,0:T(8,128)(2,1)S(1)} %broadcast_select_fusion), channel_id=1, replica_groups=mesh['row'=4,'col'=8] {'row','col'}, dimensions={0} | all-to-all | bytes 786432 | tf_op jit(solution)/shard_map/all_to_all | solution.py:21
  63.9 0.0 all-gather.3.cloned.1.call-update
  63.9 0.0 all-gather.5.cloned.1.call-start
  64.0 0.7 all-gather.5.cloned.1.call-update
  64.7 1.9 %copy.16 = f32[1,1,8,4,128,128]{4,5,2,3,1,0:T(8,128)S(1)} copy(f32[1,1,8,4,128,128]{5,4,3,2,1,0:T(8,128)} %param.9) | data formatting | bytes 4194304 | tf_op args[4]
  66.6 25.9 %all-gather.3.cloned.1.call-done = bf16[4,1536,128]{2,1,0:T(8,128)(2,1)} async-done(((bf16[1,1536,128]{2,1,0:T(8,128)(2,1)}), bf16[4,1536,128]{2,1,0:T(8,128)(2,1)}) %all-gather.3.cloned.1.call-update) | async-done | bytes 1572880 | tf_op jit(solution)/shard_map/all_gather | solution.py:23
  92.5 39.9 %all-gather.5.cloned.1.call-done = bf16[8,1536,128]{2,1,0:T(8,128)(2,1)} async-done(((bf16[1,1536,128]{2,1,0:T(8,128)(2,1)}), bf16[8,1536,128]{2,1,0:T(8,128)(2,1)}) %all-gather.5.cloned.1.call-update) | async-done | bytes 3145744 | tf_op jit(solution)/shard_map/all_gather | solution.py:26
  132.4 5.5 %bitcast_subtract_fusion = f32[1,1,8,4,128,128]{4,5,2,3,1,0:T(8,128)} fusion(f32[1,1,8,4,128,128]{4,5,2,3,1,0:T(8,128)S(1)} %copy.16, bf16[8,1536,128]{2,1,0:T(8,128)(2,1)} %all-gather.5.cloned.1.call-done, bf16[4,1536,128]{2,1,0:T(8,128)(2,1)} %all-gather.3.cloned.1.call-done), kind=kOutput, calls=%fused_computation.7 | convolution fusion | flops 1611137024 | bytes 8912896 | tf_op jit(solution)/shard_map/aik,bil->abkl/dot_general | solution.py:24
  137.9 2.9 %copy.17 = f32[1,1,8,4,128,128]{5,4,3,2,1,0:T(8,128)} copy(f32[1,1,8,4,128,128]{4,5,2,3,1,0:T(8,128)} %bitcast_subtract_fusion) | data formatting | bytes 4194304 | tf_op jit(solution)/shard_map/sub | solution.py:30
  (4 shorter events, 0.0 us)
Async XLA Ops:
  6.5 18.9 %all-to-all-start = ((bf16[8,192,128]{2,1,0:T(8,128)(2,1)}), bf16[8,192,128]{2,1,0:T(8,128)(2,1)S(1)}, u32[]{:S(2)}, u32[]{:S(2)}) async-start(bf16[8,192,128]{2,1,0:T(8,128)(2,1)} %param.5), calls=%async_computation | async-start | bytes 786432 | tf_op jit(solution)/shard_map/all_to_all | solution.py:13
  25.4 8.6 %copy-start = (s32[32]{0:T(128)S(1)}, s32[32]{0:T(128)}, u32[]{:S(2)}) copy-start(s32[32]{0:T(128)} %param.8) | copy-start | bytes 388
  30.4 17.0 %all-to-all-start.1 = ((bf16[32,48,128]{2,1,0:T(8,128)(2,1)}), bf16[32,48,128]{2,1,0:T(8,128)(2,1)S(1)}, u32[]{:S(2)}, u32[]{:S(2)}) async-start(bf16[32,48,128]{2,1,0:T(8,128)(2,1)} %bitcast.4), calls=%async_computation.1 | async-start | bytes 786432 | tf_op jit(solution)/shard_map/all_to_all | solution.py:19
  33.9 58.6 %all-gather.3.cloned.1.call-start = ((), (), s32[]{:S(2)}) async-start(), calls=%async_computation.3 | async-start | bytes 1966080 | tf_op jit(solution)/shard_map/all_gather | solution.py:23
  63.9 68.5 %all-gather.5.cloned.1.call-start = ((), (), s32[]{:S(2)}) async-start(), calls=%async_computation.4 | async-start | bytes 3538944 | tf_op jit(solution)/shard_map/all_gather | solution.py:26
Sparse Core Ops, SparseCore 0:
  64.0 28.4 all-gather.2
  94.1 38.2 all-gather.4
where the time goes:
time: 148 us
  waiting for transfers between devices  91.7 us (62%)
  blocking collectives  15.8 us (11%)
  between operations  14.1 us (10%)
  starting transfers between devices  9.97 us (7%)
  matrix products  9.54 us (6%)
  local copies, waits for them, and re-layouts  6.37 us (4%)
    all_gather x1, waiting for transfers between devices, body(): lax.all_gather(held, 'col', axis=0, tiled=True)  39.9 us
    all_gather x1, waiting for transfers between devices, body(): column_set = lax.all_gather(held, 'row', axis=0, tiled=True)  25.9 us
    all_to_all x1, blocking collectives, body(): lax.all_to_all(moved, ('row', 'col'), split_axis=0, concat_axis=0, tiled=...  15.8 us
    all_to_all x1, waiting for transfers between devices, body(): lax.all_to_all(pieces, ('row', 'col'), split_axis=0, concat_axis=0, tiled...  13.3 us
    all_to_all x1, waiting for transfers between devices, body(): lax.all_to_all(panel_right, 'col', split_axis=0, concat_axis=1, tiled=True)  11.9 us
    all_to_all x1, starting transfers between devices, body(): lax.all_to_all(panel_right, 'col', split_axis=0, concat_axis=1, tiled=True)  6.35 us
    dot_general x1, matrix products, body(): jnp.einsum('aik,bil->abkl', lax.all_gather(held, 'col', axis=0, tiled=Tru...  5.51 us
    dot_general x1, matrix products, body(): jnp.einsum('ij,bjk->bik', factor_inverse, whole, preferred_element_type=j...  4.03 us
  transfers between devices with their start and end apart: 4, of which 4 were waited for; matrix products, arithmetic and copies ran while one was open for 1% of the time, Pallas kernels for 0%

commit v1 on v0

--- a/solution.py
+++ b/solution.py
@@ -2,6 +2,12 @@
 import jax.numpy as jnp
 from jax import lax
 from jax.sharding import PartitionSpec as P
+
+
+def _connect_files(q_in, in_dim):
+    q_in = jnp.moveaxis(q_in, 0, in_dim)
+    extra = q_in.shape
+    return q_in.reshape(*extra[:in_dim], extra[in_dim] * extra[in_dim + 1], *extra[in_dim + 2 :])
 
 
 def body(panel_right, factor_inverse, ranks, owner_map, cores):
@@ -21,12 +27,32 @@
     back = lax.all_to_all(moved, ("row", "col"), split_axis=0, concat_axis=0, tiled=True)
     held = back.reshape(1, order, width)
     column_set = lax.all_gather(held, "row", axis=0, tiled=True)
-    gram = jnp.einsum(
-        "aik,bil->abkl",
-        lax.all_gather(held, "col", axis=0, tiled=True),
-        column_set,
-        preferred_element_type=jnp.float32,
-    )
+    base_arr = lax.axis_size("col")
+    local_part = lax.axis_index("col")
+    d_next, s_next, local_out = (base_arr, local_part, held.shape[0])
+    by_rank = [(to_i, (to_i + 1) % d_next) for to_i in range(d_next)]
+    all_rows = [(to_i, (to_i - 1) % d_next) for to_i in range(d_next)]
+    kept_arr = d_next // 2
+    far_arr = {}
+    w_next = arr_out = held
+    for k0 in tuple(range(kept_arr + 1)):
+        plain = lax.ppermute(w_next, axis_name="col", perm=by_rank) if k0 < kept_arr else None
+        b_now = (
+            lax.ppermute(arr_out, axis_name="col", perm=all_rows)
+            if k0 < d_next - kept_arr - 1
+            else None
+        )
+        far_arr[-k0] = jnp.einsum(
+            "aik,bil->abkl", w_next, column_set, preferred_element_type=jnp.float32
+        )
+        if 0 < k0 < d_next - kept_arr:
+            far_arr[k0] = jnp.einsum(
+                "aik,bil->abkl", arr_out, column_set, preferred_element_type=jnp.float32
+            )
+        w_next, arr_out = (plain, b_now)
+    far_arr = jnp.stack([far_arr[ii] for ii in sorted(far_arr)], 0)
+    far_arr = far_arr[(jnp.arange(d_next) - s_next + kept_arr) % d_next]
+    gram = _connect_files(far_arr, 0)
     return cores - gram[None, None]
 
 

time: 148 us -> 133 us (0.90)
  waiting for transfers between devices: 91.7 us -> 53 us
  starting transfers between devices: 9.97 us -> 21.1 us
  local copies, waits for them, and re-layouts: 6.37 us -> 11.3 us
  matrix products: 9.54 us -> 13.5 us
  other arithmetic: 0.13 us -> 3.33 us
    all_gather x1 -> x0, waiting for transfers between devices: 39.9 us -> none  [body(): lax.all_gather(held, 'col', axis=0, tiled=True)]
    ppermute x0 -> x7, waiting for transfers between devices: none -> 27.8 us  [the longest x4 22.2 us: body(): lax.ppermute(w_next, axis_name='col', perm=by_rank)]
    all_gather x1, waiting for transfers between devices: 25.9 us -> 0.01 us  [body(): column_set = lax.all_gather(held, 'row', axis=0, tiled=True)]
    ppermute x0 -> x7, starting transfers between devices: none -> 11.1 us  [the longest x3 11 us: body(): lax.ppermute(arr_out, axis_name='col', perm=all_rows)]
    dot_general x1 -> x8, matrix products: 5.51 us -> 9.51 us  [the longest x5 5.66 us: body(): jnp.einsum('aik,bil->abkl', w_next, column_set, preferred_element_type=jn...]
    gather x0 -> x1, local copies, waits for them, and re-layouts: none -> 3.61 us  [body(): far_arr = far_arr[(jnp.arange(d_next) - s_next + kept_arr) % d_next]]
    sub x0 -> x1, other arithmetic: none -> 3.18 us  [body(): return cores - gram[None, None]]
    unnamed x3 -> x9, local copies, waits for them, and re-layouts: 1.94 us -> 3.24 us
  transfers between devices with their start and end apart: 4 -> 10, of which waited for: 4 -> 8; matrix products, arithmetic and copies ran while one was open for 1% -> 7% of each run, Pallas kernels for 0% -> 0%
where the time goes in v1:
time: 133 us; the launch traced here: 132 us
  waiting for transfers between devices  53 us (40%)
  starting transfers between devices  21.1 us (16%)
  blocking collectives  15.8 us (12%)
  between operations  14.2 us (11%)
  matrix products  13.5 us (10%)
  local copies, waits for them, and re-layouts  11.3 us (8%)
  other arithmetic  3.33 us (3%)
    ppermute x4, waiting for transfers between devices, body(): lax.ppermute(w_next, axis_name='col', perm=by_rank)  22.2 us
    all_to_all x1, blocking collectives, body(): lax.all_to_all(moved, ('row', 'col'), split_axis=0, concat_axis=0, tiled=...  15.8 us
    all_to_all x1, waiting for transfers between devices, body(): lax.all_to_all(pieces, ('row', 'col'), split_axis=0, concat_axis=0, tiled...  13.3 us
    all_to_all x1, waiting for transfers between devices, body(): lax.all_to_all(panel_right, 'col', split_axis=0, concat_axis=1, tiled=True)  11.9 us
    ppermute x3, starting transfers between devices, body(): lax.ppermute(arr_out, axis_name='col', perm=all_rows)  11 us
    all_to_all x1, starting transfers between devices, body(): lax.all_to_all(panel_right, 'col', split_axis=0, concat_axis=1, tiled=True)  6.35 us
    dot_general x5, matrix products, body(): jnp.einsum('aik,bil->abkl', w_next, column_set, preferred_element_type=jn...  5.66 us
    ppermute x3, waiting for transfers between devices, body(): lax.ppermute(arr_out, axis_name='col', perm=all_rows)  5.64 us
  transfers between devices with their start and end apart: 10, of which 8 were waited for; matrix products, arithmetic and copies ran while one was open for 7% of the time, Pallas kernels for 0%

profile of v1, /device:TPU:0, one launch (start us, length us, event | category | flops | bytes accessed | tf_op | source)
XLA Modules:
  0.0 132.3 jit_solution(15430891487313819241)
XLA Ops:
  6.5 6.4 %all-to-all-start = ((bf16[8,192,128]{2,1,0:T(8,128)(2,1)}), bf16[8,192,128]{2,1,0:T(8,128)(2,1)S(1)}, u32[]{:S(2)}, u32[]{:S(2)}) async-start(bf16[8,192,128]{2,1,0:T(8,128)(2,1)} %param.5), calls=%async_computation | async-start | bytes 786432 | tf_op jit(solution)/shard_map/all_to_all | solution.py:19
  13.6 11.9 %all-to-all-done = bf16[8,192,128]{2,1,0:T(8,128)(2,1)S(1)} async-done(((bf16[8,192,128]{2,1,0:T(8,128)(2,1)}), bf16[8,192,128]{2,1,0:T(8,128)(2,1)S(1)}, u32[]{:S(2)}, u32[]{:S(2)}) %all-to-all-start) | async-done | bytes 393248 | tf_op jit(solution)/shard_map/all_to_all | solution.py:19
  25.4 0.0 copy-start.3
  25.4 4.0 %fusion.2 = bf16[1,1536,128]{1,2,0:T(8,128)(2,1)S(1)} fusion(bf16[1536,128]{1,0:T(8,128)(2,1)S(1)} %bitcast.131, bf16[1536,1536]{1,0:T(8,128)(2,1)} %param.6, pred[128]{0:T(512)(128)(4,1)S(1)} %iota_compare_fusion), kind=kOutput, calls=%fused_computation.5 | convolution fusion | flops 604372992 | bytes 5505152 | tf_op jit(solution)/shard_map/ij,bjk->bik/dot_general | solution.py:20
  29.4 0.9 copy.29
  30.4 3.5 %all-to-all-start.1 = ((bf16[32,48,128]{2,1,0:T(8,128)(2,1)}), bf16[32,48,128]{2,1,0:T(8,128)(2,1)S(1)}, u32[]{:S(2)}, u32[]{:S(2)}) async-start(bf16[32,48,128]{2,1,0:T(8,128)(2,1)} %bitcast.4), calls=%async_computation.1 | async-start | bytes 786432 | tf_op jit(solution)/shard_map/all_to_all | solution.py:25
  33.9 0.0 all-gather.2.cloned.1.call-start
  34.0 0.0 copy-done.3
  34.0 13.3 %all-to-all-done.1 = bf16[32,48,128]{2,1,0:T(8,128)(2,1)S(1)} async-done(((bf16[32,48,128]{2,1,0:T(8,128)(2,1)}), bf16[32,48,128]{2,1,0:T(8,128)(2,1)S(1)}, u32[]{:S(2)}, u32[]{:S(2)}) %all-to-all-start.1) | async-done | bytes 393248 | tf_op jit(solution)/shard_map/all_to_all | solution.py:25
  47.3 0.6 gather_fusion
  48.0 0.1 broadcast_select_fusion
  48.1 15.8 %all_to_all.19 = bf16[32,48,128]{2,1,0:T(8,128)(2,1)} all-to-all(bf16[32,48,128]{2,1,0:T(8,128)(2,1)S(1)} %broadcast_select_fusion), channel_id=1, replica_groups=mesh['row'=4,'col'=8] {'row','col'}, dimensions={0} | all-to-all | bytes 786432 | tf_op jit(solution)/shard_map/all_to_all | solution.py:27
  63.9 0.0 all-gather.2.cloned.1.call-update
  63.9 0.2 collective-permute-start
  64.1 9.1 %collective-permute-done = bf16[1,1536,128]{2,1,0:T(8,128)(2,1)S(1)} collective-permute-done((bf16[1,1536,128]{2,1,0:T(8,128)(2,1)}, bf16[1,1536,128]{2,1,0:T(8,128)(2,1)S(1)}, u32[]{:S(2)}, u32[]{:S(2)}) %collective-permute-start) | collective-permute-done | bytes 393248 | tf_op jit(solution)/shard_map/ppermute | solution.py:39
  73.2 0.0 collective-permute-start.1
  73.2 3.5 %collective-permute-start.4 = (bf16[1,1536,128]{2,1,0:T(8,128)(2,1)}, bf16[1,1536,128]{2,1,0:T(8,128)(2,1)S(1)}, u32[]{:S(2)}, u32[]{:S(2)}) collective-permute-start(bf16[1,1536,128]{2,1,0:T(8,128)(2,1)} %bitcast.128), channel_id=1, source_target_pairs={{0,7},{1,0},{2,1},{3,2},{4,3},{5,4},{6,5},{7,6},{8,15},{9,8},{10,9... | collective-permute-start | bytes 1179656 | tf_op jit(solution)/shard_map/ppermute | solution.py:41
  76.7 6.5 %collective-permute-done.1 = bf16[1,1536,128]{2,1,0:T(8,128)(2,1)S(1)} collective-permute-done((bf16[1,1536,128]{2,1,0:T(8,128)(2,1)S(1)}, bf16[1,1536,128]{2,1,0:T(8,128)(2,1)S(1)}, u32[]{:S(2)}, u32[]{:S(2)}) %collective-permute-start.1) | collective-permute-done | bytes 393248 | tf_op jit(solution)/shard_map/ppermute | solution.py:39
  83.2 0.0 collective-permute-start.2
  83.2 2.3 %collective-permute-done.4 = bf16[1,1536,128]{2,1,0:T(8,128)(2,1)S(1)} collective-permute-done((bf16[1,1536,128]{2,1,0:T(8,128)(2,1)}, bf16[1,1536,128]{2,1,0:T(8,128)(2,1)S(1)}, u32[]{:S(2)}, u32[]{:S(2)}) %collective-permute-start.4) | collective-permute-done | bytes 393248 | tf_op jit(solution)/shard_map/ppermute | solution.py:41
  85.6 3.6 %collective-permute-start.5 = (bf16[1,1536,128]{2,1,0:T(8,128)(2,1)S(1)}, bf16[1,1536,128]{2,1,0:T(8,128)(2,1)}, u32[]{:S(2)}, u32[]{:S(2)}) collective-permute-start(bf16[1,1536,128]{2,1,0:T(8,128)(2,1)S(1)} %collective-permute-done.4), channel_id=1, source_target_pairs={{0,7},{1,0},{2,1},{3,2},{4,3},{5,4},{6,5},{7,6},{8,15},{9,8},{10,9... | collective-permute-start | bytes 1179656 | tf_op jit(solution)/shard_map/ppermute | solution.py:41
  89.2 3.8 %collective-permute-done.2 = bf16[1,1536,128]{2,1,0:T(8,128)(2,1)} collective-permute-done((bf16[1,1536,128]{2,1,0:T(8,128)(2,1)S(1)}, bf16[1,1536,128]{2,1,0:T(8,128)(2,1)}, u32[]{:S(2)}, u32[]{:S(2)}) %collective-permute-start.2) | collective-permute-done | bytes 393248 | tf_op jit(solution)/shard_map/ppermute | solution.py:39
  93.0 0.0 collective-permute-start.3
  93.0 1.9 %copy.38 = f32[1,1,8,4,128,128]{4,5,3,2,1,0:T(8,128)S(1)} copy(f32[1,1,8,4,128,128]{5,4,3,2,1,0:T(8,128)} %param.9) | data formatting | bytes 4194304 | tf_op args[4]
  94.9 3.3 %collective-permute-done.5 = bf16[1,1536,128]{2,1,0:T(8,128)(2,1)} collective-permute-done((bf16[1,1536,128]{2,1,0:T(8,128)(2,1)S(1)}, bf16[1,1536,128]{2,1,0:T(8,128)(2,1)}, u32[]{:S(2)}, u32[]{:S(2)}) %collective-permute-start.5) | collective-permute-done | bytes 393248 | tf_op jit(solution)/shard_map/ppermute | solution.py:41
  98.2 3.8 %collective-permute-start.6 = (bf16[1,1536,128]{2,1,0:T(8,128)(2,1)}, bf16[1,1536,128]{2,1,0:T(8,128)(2,1)}, u32[]{:S(2)}, u32[]{:S(2)}) collective-permute-start(bf16[1,1536,128]{2,1,0:T(8,128)(2,1)} %collective-permute-done.5), channel_id=1, source_target_pairs={{0,7},{1,0},{2,1},{3,2},{4,3},{5,4},{6,5},{7,6},{8,15},{9,8},{10,9... | collective-permute-start | bytes 1179656 | tf_op jit(solution)/shard_map/ppermute | solution.py:41
  102.0 2.8 %collective-permute-done.3 = bf16[1,1536,128]{2,1,0:T(8,128)(2,1)} collective-permute-done((bf16[1,1536,128]{2,1,0:T(8,128)(2,1)}, bf16[1,1536,128]{2,1,0:T(8,128)(2,1)}, u32[]{:S(2)}, u32[]{:S(2)}) %collective-permute-start.3) | collective-permute-done | bytes 393248 | tf_op jit(solution)/shard_map/ppermute | solution.py:39
  104.8 0.0 all-gather.2.cloned.1.call-done
  104.8 0.0 copy-start
  104.8 2.2 %fusion.10 = f32[8,1,4,128,128]{3,4,2,1,0:T(8,128)S(1)} fusion(bf16[4,1536,128]{2,1,0:T(8,128)(2,1)} %all-gather.2.cloned.1.call-done, bf16[1,1536,128]{2,1,0:T(8,128)(2,1)} %collective-permute-done.3), kind=kOutput, calls=%fused_computation.22 | convolution fusion | flops 201326592 | bytes 2228224 | tf_op jit(solution)/shard_map/aik,bil->abkl/dot_general | solution.py:45
  107.0 0.0 copy-done
  107.0 1.6 %fusion.9 = f32[8,1,4,128,128]{3,4,2,1,0:T(8,128)S(1)} fusion(f32[8,1,4,128,128]{3,4,2,1,0:T(8,128)S(1)} %fusion.10, bf16[4,1536,128]{2,1,0:T(8,128)(2,1)S(1)} %copy-done, bf16[1,1536,128]{2,1,0:T(8,128)(2,1)} %collective-permute-done.2), kind=kOutput, calls=%fused_computation.20 | convolution fusion | flops 201326592 | bytes 2228224 | tf_op jit(solution)/shard_map/aik,bil->abkl/dot_general | solution.py:45
  108.7 0.0 copy-start.1
  108.7 0.6 fusion.8
  109.3 0.6 fusion.7
  109.9 0.0 copy-done.1
  109.9 0.6 fusion.6
  110.6 0.6 fusion.5
  111.2 1.6 %fusion.4 = f32[8,1,4,128,128]{3,4,2,1,0:T(8,128)S(1)} fusion(f32[8,1,4,128,128]{3,4,2,1,0:T(8,128)S(1)} %fusion.5, bf16[4,1536,128]{2,1,0:T(8,128)(2,1)S(1)} %copy-done, bf16[1,1536,128]{2,1,0:T(8,128)(2,1)} %collective-permute-done.5), kind=kOutput, calls=%fused_computation.10 | convolution fusion | flops 201326592 | bytes 2228224 | tf_op jit(solution)/shard_map/aik,bil->abkl/dot_general | solution.py:49
  112.8 0.0 collective-permute-done.6
  112.8 1.6 %fusion.3 = f32[8,1,4,128,128]{3,4,2,1,0:T(8,128)S(1)} fusion(f32[8,1,4,128,128]{3,4,2,1,0:T(8,128)S(1)} %fusion.4, bf16[4,1536,128]{2,1,0:T(8,128)(2,1)S(1)} %copy-done, bf16[1,1536,128]{2,1,0:T(8,128)(2,1)} %collective-permute-done.6), kind=kOutput, calls=%fused_computation.8 | convolution fusion | flops 201326592 | bytes 2228224 | tf_op jit(solution)/shard_map/aik,bil->abkl/dot_general | solution.py:49
  114.4 0.0 copy-start.2
  114.4 1.3 copy-done.2
  115.8 3.6 %gather_fusion.1 = f32[8,4,128,128]{2,3,1,0:T(8,128)} fusion(f32[8,4,128,128]{2,3,1,0:T(8,128)} %bitcast.130, s32[1024]{0:T(1024)S(1)} %pad_clamp_fusion), kind=kCustom, calls=%fused_computation.1 | custom fusion | bytes 4194336 | tf_op jit(solution)/shard_map/gather | solution.py:54
  119.4 3.2 %bitcast_subtract_fusion = f32[1,1,8,4,128,128]{4,5,3,2,1,0:T(8,128)} fusion(f32[1,1,8,4,128,128]{4,5,3,2,1,0:T(8,128)S(1)} %copy.38, f32[8,4,128,128]{2,3,1,0:T(8,128)} %gather_fusion.1), kind=kLoop, calls=%fused_computation.6 | loop fusion | flops 524288 | bytes 6291456 | tf_op jit(solution)/shard_map/sub | solution.py:56
  122.5 2.9 %copy.39 = f32[1,1,8,4,128,128]{5,4,3,2,1,0:T(8,128)} copy(f32[1,1,8,4,128,128]{4,5,3,2,1,0:T(8,128)} %bitcast_subtract_fusion) | data formatting | bytes 4194304 | tf_op jit(solution)/shard_map/sub | solution.py:56
  (6 shorter events, 0.0 us)
Async XLA Ops:
  6.5 18.9 %all-to-all-start = ((bf16[8,192,128]{2,1,0:T(8,128)(2,1)}), bf16[8,192,128]{2,1,0:T(8,128)(2,1)S(1)}, u32[]{:S(2)}, u32[]{:S(2)}) async-start(bf16[8,192,128]{2,1,0:T(8,128)(2,1)} %param.5), calls=%async_computation | async-start | bytes 786432 | tf_op jit(solution)/shard_map/all_to_all | solution.py:19
  25.4 8.6 %copy-start.3 = (s32[32]{0:T(128)S(1)}, s32[32]{0:T(128)}, u32[]{:S(2)}) copy-start(s32[32]{0:T(128)} %param.8) | copy-start | bytes 388
  30.4 17.0 %all-to-all-start.1 = ((bf16[32,48,128]{2,1,0:T(8,128)(2,1)}), bf16[32,48,128]{2,1,0:T(8,128)(2,1)S(1)}, u32[]{:S(2)}, u32[]{:S(2)}) async-start(bf16[32,48,128]{2,1,0:T(8,128)(2,1)} %bitcast.4), calls=%async_computation.1 | async-start | bytes 786432 | tf_op jit(solution)/shard_map/all_to_all | solution.py:25
  33.9 70.9 %all-gather.2.cloned.1.call-start = ((), (), s32[]{:S(2)}) async-start(), calls=%async_computation.3 | async-start | bytes 1966080 | tf_op jit(solution)/shard_map/all_gather | solution.py:29
  63.9 9.3 %collective-permute-start = (bf16[1,1536,128]{2,1,0:T(8,128)(2,1)}, bf16[1,1536,128]{2,1,0:T(8,128)(2,1)S(1)}, u32[]{:S(2)}, u32[]{:S(2)}) collective-permute-start(bf16[1,1536,128]{2,1,0:T(8,128)(2,1)} %bitcast.127), channel_id=1, source_target_pairs={{0,1},{1,2},{2,3},{3,4},{4,5},{5,6},{6,7},{7,0},{8,9},{9,10},{10,1... | collective-permute-start | bytes 1179656 | tf_op jit(solution)/shard_map/ppermute | solution.py:39
  73.2 10.0 %collective-permute-start.1 = (bf16[1,1536,128]{2,1,0:T(8,128)(2,1)S(1)}, bf16[1,1536,128]{2,1,0:T(8,128)(2,1)S(1)}, u32[]{:S(2)}, u32[]{:S(2)}) collective-permute-start(bf16[1,1536,128]{2,1,0:T(8,128)(2,1)S(1)} %collective-permute-done), channel_id=1, source_target_pairs={{0,1},{1,2},{2,3},{3,4},{4,5},{5,6},{6,7},{7,0},{8,9},{9,10},{10,1... | collective-permute-start | bytes 1179656 | tf_op jit(solution)/shard_map/ppermute | solution.py:39
  73.2 12.4 %collective-permute-start.4 = (bf16[1,1536,128]{2,1,0:T(8,128)(2,1)}, bf16[1,1536,128]{2,1,0:T(8,128)(2,1)S(1)}, u32[]{:S(2)}, u32[]{:S(2)}) collective-permute-start(bf16[1,1536,128]{2,1,0:T(8,128)(2,1)} %bitcast.128), channel_id=1, source_target_pairs={{0,7},{1,0},{2,1},{3,2},{4,3},{5,4},{6,5},{7,6},{8,15},{9,8},{10,9... | collective-permute-start | bytes 1179656 | tf_op jit(solution)/shard_map/ppermute | solution.py:41
  83.2 9.8 %collective-permute-start.2 = (bf16[1,1536,128]{2,1,0:T(8,128)(2,1)S(1)}, bf16[1,1536,128]{2,1,0:T(8,128)(2,1)}, u32[]{:S(2)}, u32[]{:S(2)}) collective-permute-start(bf16[1,1536,128]{2,1,0:T(8,128)(2,1)S(1)} %collective-permute-done.1), channel_id=1, source_target_pairs={{0,1},{1,2},{2,3},{3,4},{4,5},{5,6},{6,7},{7,0},{8,9},{9,10},{10,1... | collective-permute-start | bytes 1179656 | tf_op jit(solution)/shard_map/ppermute | solution.py:39
  85.6 12.7 %collective-permute-start.5 = (bf16[1,1536,128]{2,1,0:T(8,128)(2,1)S(1)}, bf16[1,1536,128]{2,1,0:T(8,128)(2,1)}, u32[]{:S(2)}, u32[]{:S(2)}) collective-permute-start(bf16[1,1536,128]{2,1,0:T(8,128)(2,1)S(1)} %collective-permute-done.4), channel_id=1, source_target_pairs={{0,7},{1,0},{2,1},{3,2},{4,3},{5,4},{6,5},{7,6},{8,15},{9,8},{10,9... | collective-permute-start | bytes 1179656 | tf_op jit(solution)/shard_map/ppermute | solution.py:41
  93.0 11.9 %collective-permute-start.3 = (bf16[1,1536,128]{2,1,0:T(8,128)(2,1)}, bf16[1,1536,128]{2,1,0:T(8,128)(2,1)}, u32[]{:S(2)}, u32[]{:S(2)}) collective-permute-start(bf16[1,1536,128]{2,1,0:T(8,128)(2,1)} %collective-permute-done.2), channel_id=1, source_target_pairs={{0,1},{1,2},{2,3},{3,4},{4,5},{5,6},{6,7},{7,0},{8,9},{9,10},{10,1... | collective-permute-start | bytes 1179656 | tf_op jit(solution)/shard_map/ppermute | solution.py:39
  98.2 14.6 %collective-permute-start.6 = (bf16[1,1536,128]{2,1,0:T(8,128)(2,1)}, bf16[1,1536,128]{2,1,0:T(8,128)(2,1)}, u32[]{:S(2)}, u32[]{:S(2)}) collective-permute-start(bf16[1,1536,128]{2,1,0:T(8,128)(2,1)} %collective-permute-done.5), channel_id=1, source_target_pairs={{0,7},{1,0},{2,1},{3,2},{4,3},{5,4},{6,5},{7,6},{8,15},{9,8},{10,9... | collective-permute-start | bytes 1179656 | tf_op jit(solution)/shard_map/ppermute | solution.py:41
  104.8 2.2 %copy-start = (bf16[4,1536,128]{2,1,0:T(8,128)(2,1)S(1)}, bf16[4,1536,128]{2,1,0:T(8,128)(2,1)}, u32[]{:S(2)}) copy-start(bf16[4,1536,128]{2,1,0:T(8,128)(2,1)} %all-gather.2.cloned.1.call-done) | copy-start | bytes 4718596
  108.7 1.3 copy-start.1
  114.4 1.3 copy-start.2
Sparse Core Ops, SparseCore 0:
  64.0 28.4 all-gather.1
